TPU v7x, 256 devices: a whole 4x4x8 slice. The times are simulated.
256 devices in a mesh: energy: 16 (over z, core), cell: 16 (over y, x).
Axes of the slice: x: 4, y: 4, z: 8, core: 2. Of those that a mesh axis runs over, the one named last changes fastest.
Arguments:
- green: bfloat16 [4, 96, 32, 16, 512], P(None, 'energy', 'cell'), may hold values from -6 to 6
- screened: bfloat16 [4, 96, 32, 16, 512], P(None, 'energy', None, 'cell'), may hold values from -6 to 6
- cell_map: int32 [32], replicated, may hold values from 0 to 31, each once
- shift_table: int32 [16, 16, 3], replicated, may hold values from 0 to 5, as said below
- shift_count: int32 [16, 16], replicated, may hold values from 1 to 3, as said below
Outputs:
- sigma: float32 [4, 96, 32, 16, 512], P(None, 'energy', 'cell')
Inputs may be any that keep to these rules, and one draw needn't show every extreme that they name: `shift_table`: offsets of requested energies within the source group; slots c >= shift_count[g, s] are not read. `shift_count`: some destination group requests 3 energies from every source group. `cell_map`: each cell stands at exactly one position.
All inputs are finite; a program needn't handle non-finite values.
Results may differ from a plain program's by a relative error of at most 0.0003.
Values may be sent and summed in bfloat16 or wider, within the bound.
A program may use at most 128 MiB of HBM per device.

v0:
```python
import jax
import jax.numpy as jnp
from jax import lax
from jax.sharding import PartitionSpec as P

SCALE = 0.2


def per_device(green, screened, cell_map, shift_table, shift_count):
    groups = lax.axis_size("energy")
    cell_count = lax.axis_size("cell")
    per_energy = green.shape[1]
    per_cell = green.shape[2]
    width = green.shape[4]
    slot_count = shift_table.shape[2]
    wanted = jnp.transpose(cell_map.reshape(cell_count, per_cell)).reshape(-1)
    outgoing = jnp.take(screened, wanted, axis=2)
    outgoing = outgoing.reshape(4, per_energy, per_cell, cell_count, screened.shape[3], width)
    arrived = lax.all_to_all(outgoing, "cell", split_axis=3, concat_axis=3, tiled=True)
    owned = arrived.reshape(4, per_energy, per_cell, green.shape[3], width)
    whole = lax.all_gather(green, "energy", axis=1, tiled=True)
    padding = jnp.zeros((4, per_energy) + whole.shape[2:], whole.dtype)
    padded = jnp.concatenate([padding, whole], axis=1)
    group = lax.axis_index("energy")
    first = group * per_energy
    table_row = shift_table[group]
    counts = shift_count[group]
    every = lax.all_gather(owned, "energy", axis=1, tiled=True)

    def values_of(energy):
        return lax.dynamic_index_in_dim(every, energy, 1, keepdims=False)

    def turn(totals, source):
        sums = list(totals)
        for slot in range(slot_count):
            energy = source * per_energy + table_row[source, slot]
            live = (slot < counts[source]).astype(jnp.float32)
            start = jnp.maximum(first - energy, -per_energy) + per_energy
            window = lax.dynamic_slice_in_dim(padded, start, per_energy, 1)
            value = values_of(energy)
            for kind in range(2):
                g_real = window[2 * kind].astype(jnp.float32)
                g_imag = window[2 * kind + 1].astype(jnp.float32)
                w_real = value[2 * kind].astype(jnp.float32)[None] * live
                w_imag = value[2 * kind + 1].astype(jnp.float32)[None] * live
                sums[2 * kind] = sums[2 * kind] - (g_real * w_imag + g_imag * w_real)
                sums[2 * kind + 1] = sums[2 * kind + 1] + (g_real * w_real - g_imag * w_imag)
        return (tuple(sums), None)

    zeros = jnp.zeros(green.shape[1:], jnp.float32)
    totals, _ = lax.scan(turn, (zeros, zeros, zeros, zeros), jnp.arange(groups, dtype=jnp.int32))
    return jnp.stack(totals, axis=0) * SCALE


def solution(mesh):
    placed = (
        P(None, "energy", "cell", None, None),
        P(None, "energy", None, "cell", None),
        P(),
        P(),
        P(),
    )
    return jax.shard_map(
        per_device,
        mesh=mesh,
        in_specs=placed,
        out_specs=P(None, "energy", "cell", None, None),
        check_vma=False,
    )
```

profile of v0, /device:TPU:1, one launch (start us, length us, event | category | flops | bytes accessed | tf_op | source)
XLA Modules:
  0.0 408.6 jit_solution(6469236370796020394)
XLA Ops:
  12.3 21.0 %all_to_all.5 = bf16[4,6,2,16,1,512]{5,2,1,0,4,3:T(2,128)(2,1)} all-to-all(bf16[4,6,2,16,1,512]{5,2,1,0,4,3:T(2,128)(2,1)S(1)} %broadcast_select_fusion), channel_id=1, replica_groups=mesh['energy'=16,'cell'=16] {'cell'}, dimensions={3} | all-to-all | bytes 1572864 | tf_op jit(solution)/shard_map/all_to_all | solution.py:19
  34.1 55.1 %all-gather.4.cloned.1.call-done = bf16[4,96,2,16,512]{4,3,2,1,0:T(8,128)(2,1)} async-done(((bf16[4,6,2,16,512]{4,3,2,1,0:T(8,128)(2,1)}), bf16[4,96,2,16,512]{4,3,2,1,0:T(8,128)(2,1)}) %all-gather.4.cloned.1.call-update) | async-done | bytes 12582928 | tf_op jit(solution)/shard_map/all_gather | solution.py:21
  89.1 11.3 %concatenate.3 = bf16[4,102,2,16,512]{4,3,2,1,0:T(8,128)(2,1)} pad(bf16[4,96,2,16,512]{4,3,2,1,0:T(8,128)(2,1)} %all-gather.4.cloned.1.call-done, bf16[]{:T(256)} %constant.96.clone.1), padding=0_0x6_0x0_0x0_0x0_0 | pad | bytes 25952258 | tf_op jit(solution)/shard_map/concatenate | solution.py:23
  100.5 64.7 %all-gather.6.cloned.1.call-done = bf16[4,96,2,16,1,512]{5,2,1,0,4,3:T(2,128)(2,1)} async-done(((bf16[4,6,2,16,1,512]{5,2,1,0,4,3:T(2,128)(2,1)}), bf16[4,96,2,16,1,512]{5,2,1,0,4,3:T(2,128)(2,1)}) %all-gather.6.cloned.1.call-update) | async-done | bytes 12582928 | tf_op jit(solution)/shard_map/all_gather | solution.py:28
  165.2 23.7 %copy.15 = bf16[4,96,2,16,512]{4,3,2,1,0:T(8,128)(2,1)} copy(bf16[4,96,2,16,512]{4,2,1,0,3:T(2,128)(2,1)} %bitcast.179) | data formatting | bytes 25165824
  188.9 211.5 %while.20 = (s32[]{:T(128)}, f32[6,2,16,512]{3,2,1,0:T(8,128)S(1)}, f32[6,2,16,512]{3,2,1,0:T(8,128)S(1)}, f32[6,2,16,512]{3,2,1,0:T(8,128)S(1)}, f32[6,2,16,512...) while((s32[]{:T(128)}, f32[6,2,16,512]{3,2,1,0:T(8,128)S(1)}, ...), condition=%wide.region_1.2_spmd.clone, body=%wide.region_0.1_spmd.clone.sunk | while | flops 6684718 | bytes 7471924 | solution.py:51
  198.6 1.8 fusion.28
  200.4 1.8 fusion.27
  211.8 1.8 fusion.28
  213.6 1.8 fusion.27
  225.0 1.8 fusion.28
  238.2 1.8 fusion.28
  251.4 1.8 fusion.28
  264.7 1.8 fusion.28
  277.9 1.8 fusion.28
  291.1 1.8 fusion.28
  304.3 1.8 fusion.28
  317.5 1.8 fusion.28
  330.7 1.8 fusion.28
  344.0 1.8 fusion.28
  357.2 1.8 fusion.28
  370.4 1.8 fusion.28
  383.6 1.8 fusion.28
  396.8 1.8 fusion.28
  (102 shorter events, 81.1 us)
Async XLA Ops:
  6.5 26.8 %copy-start = (s32[16,16,3]{1,0,2:T(8,128)S(1)}, s32[16,16,3]{1,0,2:T(8,128)}, u32[]{:S(2)}) copy-start(s32[16,16,3]{1,0,2:T(8,128)} %param.10) | copy-start | bytes 9220
  6.5 82.6 %all-gather.4.cloned.1.call-start = ((), (), s32[]{:S(2)}) async-start(), calls=%async_computation.1 | async-start | bytes 13369344 | tf_op jit(solution)/shard_map/all_gather | solution.py:21
  7.3 157.9 %all-gather.6.cloned.1.call-start = ((), (), s32[]{:S(2)}) async-start(), calls=%async_computation.2 | async-start | bytes 13369344 | tf_op jit(solution)/shard_map/all_gather | solution.py:28
Sparse Core Ops, SparseCore 0:
  9.2 79.8 all-gather.3
  91.0 74.1 all-gather.5
where the time goes:
time: 413 us; the launch traced here: 409 us
  waiting for transfers between devices  121 us (29%)
  loops' own time  106 us (26%)
  other arithmetic  76.4 us (18%)
  local copies, waits for them, and re-layouts  71.2 us (17%)
  blocking collectives  21 us (5%)
  between operations  13.5 us (3%)
    another operation x1, loops' own time, per_device(): lax.scan(turn, (zeros, zeros, zeros, zeros), jnp.arange(groups, dtype=jnp...  106 us
    all_gather x1, waiting for transfers between devices, per_device(): every = lax.all_gather(owned, 'energy', axis=1, tiled=True)  64.7 us
    add x32, other arithmetic, turn(): sums[2 * kind + 1] + (g_real * w_real - g_imag * w_imag)  57.2 us
    all_gather x1, waiting for transfers between devices, per_device(): whole = lax.all_gather(green, 'energy', axis=1, tiled=True)  55.1 us
    unnamed x5, local copies, waits for them, and re-layouts  25.5 us
    all_to_all x1, blocking collectives, per_device(): lax.all_to_all(outgoing, 'cell', split_axis=3, concat_axis=3, tiled=True)  21 us
    mul x16, other arithmetic, turn(): w_imag = value[2 * kind + 1].astype(jnp.float32)[None] * live  16.8 us
    concatenate x1, local copies, waits for them, and re-layouts, per_device(): padded = jnp.concatenate([padding, whole], axis=1)  11.3 us
  transfers between devices with their start and end apart: 2, of which 2 were waited for; matrix products, arithmetic and copies ran while one was open for 4% of the time, Pallas kernels for 0%

commit v1 on v0

--- a/solution.py
+++ b/solution.py
@@ -4,6 +4,22 @@
 from jax.sharding import PartitionSpec as P
 
 SCALE = 0.2
+
+
+def pairwise_exchange(x, axis, split, join):
+    ways, here = (lax.axis_size(axis), lax.axis_index(axis))
+    width = x.shape[split] // ways
+    dims = list(x.shape)
+    dims[split] = width
+    height = dims[join]
+    dims[join] = height * ways
+    full = jnp.zeros(dims, x.dtype)
+    for mask in range(ways):
+        part = lax.dynamic_slice_in_dim(x, (here ^ mask) * width, width, axis=split)
+        if mask:
+            part = lax.ppermute(part, axis, [(d, d ^ mask) for d in range(ways)])
+        full = lax.dynamic_update_slice_in_dim(full, part, (here ^ mask) * height, axis=join)
+    return full
 
 
 def per_device(green, screened, cell_map, shift_table, shift_count):
@@ -16,7 +32,7 @@
     wanted = jnp.transpose(cell_map.reshape(cell_count, per_cell)).reshape(-1)
     outgoing = jnp.take(screened, wanted, axis=2)
     outgoing = outgoing.reshape(4, per_energy, per_cell, cell_count, screened.shape[3], width)
-    arrived = lax.all_to_all(outgoing, "cell", split_axis=3, concat_axis=3, tiled=True)
+    arrived = pairwise_exchange(outgoing, "cell", 3, 3)
     owned = arrived.reshape(4, per_energy, per_cell, green.shape[3], width)
     whole = lax.all_gather(green, "energy", axis=1, tiled=True)
     padding = jnp.zeros((4, per_energy) + whole.shape[2:], whole.dtype)

time: 413 us -> 387 us (0.937)
  starting transfers between devices: 0.04 us -> 29.3 us
  waiting for transfers between devices: 121 us -> 95.3 us
  blocking collectives: 21 us -> 0 us
  local copies, waits for them, and re-layouts: 71.2 us -> 62.8 us
    all_gather x1, waiting for transfers between devices: 55.1 us -> 22.6 us  [per_device(): whole = lax.all_gather(green, 'energy', axis=1, tiled=True)]
    ppermute x0 -> x15, starting transfers between devices: none -> 29.3 us  [pairwise_exchange(): part = lax.ppermute(part, axis, [(d, d ^ mask) for d in range(ways)])]
    unnamed x5 -> x6, local copies, waits for them, and re-layouts: 25.5 us -> 2.64 us
    all_to_all x1 -> x0, blocking collectives: 21 us -> none  [per_device(): lax.all_to_all(outgoing, 'cell', split_axis=3, concat_axis=3, tiled=True)]
    dynamic_update_slice x0 -> x16, local copies, waits for them, and re-layouts: none -> 13.8 us  [pairwise_exchange(): lax.dynamic_update_slice_in_dim(full, part, (here ^ mask) * height, axis=...]
    ppermute x0 -> x15, waiting for transfers between devices: none -> 7.29 us  [pairwise_exchange(): part = lax.ppermute(part, axis, [(d, d ^ mask) for d in range(ways)])]
  transfers between devices with their start and end apart: 2 -> 17, of which waited for: 2 -> 3; matrix products, arithmetic and copies ran while one was open for 4% -> 9% of each run, Pallas kernels for 0% -> 0%
where the time goes in v1:
time: 387 us; the launch traced here: 383 us
  loops' own time  105 us (27%)
  waiting for transfers between devices  95.3 us (25%)
  other arithmetic  76.1 us (20%)
  local copies, waits for them, and re-layouts  62.8 us (16%)
  starting transfers between devices  29.3 us (8%)
  between operations  13.9 us (4%)
    another operation x1, loops' own time, per_device(): lax.scan(turn, (zeros, zeros, zeros, zeros), jnp.arange(groups, dtype=jnp...  105 us
    all_gather x1, waiting for transfers between devices, per_device(): every = lax.all_gather(owned, 'energy', axis=1, tiled=True)  64.7 us
    add x32, other arithmetic, turn(): sums[2 * kind + 1] + (g_real * w_real - g_imag * w_imag)  57.8 us
    ppermute x15, starting transfers between devices, pairwise_exchange(): part = lax.ppermute(part, axis, [(d, d ^ mask) for d in range(ways)])  29.3 us
    all_gather x1, waiting for transfers between devices, per_device(): whole = lax.all_gather(green, 'energy', axis=1, tiled=True)  22.6 us
    mul x16, other arithmetic, turn(): w_imag = value[2 * kind + 1].astype(jnp.float32)[None] * live  16.9 us
    dynamic_update_slice x16, local copies, waits for them, and re-layouts, pairwise_exchange(): lax.dynamic_update_slice_in_dim(full, part, (here ^ mask) * height, axis=...  13.8 us
    concatenate x1, local copies, waits for them, and re-layouts, per_device(): padded = jnp.concatenate([padding, whole], axis=1)  11.4 us
  transfers between devices with their start and end apart: 17, of which 3 were waited for; matrix products, arithmetic and copies ran while one was open for 9% of the time, Pallas kernels for 0%

profile of v1, /device:TPU:1, one launch (start us, length us, event | category | flops | bytes accessed | tf_op | source)
XLA Modules:
  0.0 382.7 jit_solution(8435021029583829166)
XLA Ops:
  11.9 2.3 constant_dynamic-slice_fusion.4
  14.2 6.3 %collective-permute-start.9 = (bf16[4,6,2,1,1,512]{5,3,2,1,0,4:T(2,128)(2,1)S(1)}, bf16[4,6,2,1,1,512]{5,3,2,1,0,4:T(2,128)(2,1)S(1)}, u32[]{:S(2)}, u32[]{:S(2)}) collective-permute-start(bf16[4,6,2,1,1,512]{5,3,2,1,0,4:T(2,128)(2,1)S(1)} %get-tuple-element.260), channel_id=1, source_target_pairs={{0,10},{1,11},{2,8},{3,9},{4,14},{5,15},{6,12},{7,13},{8,2},{9,3},... | collective-permute-start | bytes 147464 | tf_op jit(solution)/shard_map/ppermute | solution.py:20
  20.6 2.9 collective-permute-start.7
  23.8 3.5 collective-permute-start.5
  28.9 7.3 %collective-permute-done.7 = bf16[4,6,2,1,1,512]{5,3,2,1,0,4:T(2,128)(2,1)S(1)} collective-permute-done((bf16[4,6,2,1,1,512]{5,3,2,1,0,4:T(2,128)(2,1)S(1)}, bf16[4,6,2,1,1,512]{5,3,2,1,0,4:T(2,128)(2,1)S(1)}, u32[]{:S(2)}, u32[]{:S(2)}) %collective-permute-start.7) | collective-permute-done | bytes 49184 | tf_op jit(solution)/shard_map/ppermute | solution.py:20
  39.4 3.1 collective-permute-start.10
  45.1 2.5 collective-permute-start.13
  47.6 3.2 collective-permute-start.14
  66.5 22.6 %all-gather.3.cloned.1.call-done = bf16[4,96,2,16,512]{4,3,2,1,0:T(8,128)(2,1)} async-done(((bf16[4,6,2,16,512]{4,3,2,1,0:T(8,128)(2,1)}), bf16[4,96,2,16,512]{4,3,2,1,0:T(8,128)(2,1)}) %all-gather.3.cloned.1.call-update) | async-done | bytes 12582928 | tf_op jit(solution)/shard_map/all_gather | solution.py:37
  89.1 11.4 %concatenate.3 = bf16[4,102,2,16,512]{4,3,2,1,0:T(8,128)(2,1)} pad(bf16[4,96,2,16,512]{4,3,2,1,0:T(8,128)(2,1)} %all-gather.3.cloned.1.call-done, bf16[]{:T(256)} %constant.129.clone.1), padding=0_0x6_0x0_0x0_0x0_0 | pad | bytes 25952258 | tf_op jit(solution)/shard_map/concatenate | solution.py:39
  100.5 64.7 %all-gather.5.cloned.1.call-done = bf16[4,96,2,16,512]{4,3,2,1,0:T(8,128)(2,1)} async-done(((bf16[4,6,2,16,512]{4,3,2,1,0:T(8,128)(2,1)}), bf16[4,96,2,16,512]{4,3,2,1,0:T(8,128)(2,1)}) %all-gather.5.cloned.1.call-update) | async-done | bytes 12582928 | tf_op jit(solution)/shard_map/all_gather | solution.py:44
  165.2 209.3 %while.20 = (s32[]{:T(128)}, f32[6,2,16,512]{3,2,1,0:T(8,128)S(1)}, f32[6,2,16,512]{3,2,1,0:T(8,128)S(1)}, f32[6,2,16,512]{3,2,1,0:T(8,128)S(1)}, f32[6,2,16,512...) while((s32[]{:T(128)}, f32[6,2,16,512]{3,2,1,0:T(8,128)S(1)}, ...), condition=%wide.region_1.2_spmd.clone, body=%wide.region_0.1_spmd.clone.sunk | while | flops 6684718 | bytes 7471932 | solution.py:67
  174.6 1.9 fusion.28
  202.6 1.8 fusion.29
  215.7 1.8 fusion.29
  228.8 1.8 fusion.29
  241.9 1.8 fusion.29
  254.9 1.8 fusion.29
  268.1 1.8 fusion.29
  281.1 1.8 fusion.29
  294.2 1.8 fusion.29
  307.3 1.8 fusion.29
  359.6 1.8 fusion.29
  372.7 1.8 fusion.29
  (152 shorter events, 112.0 us)
Async XLA Ops:
  6.5 59.3 %copy-start = (s32[16,16,3]{1,0,2:T(8,128)S(1)}, s32[16,16,3]{1,0,2:T(8,128)}, u32[]{:S(2)}) copy-start(s32[16,16,3]{1,0,2:T(8,128)} %param.10) | copy-start | bytes 9220
  6.5 82.6 %all-gather.3.cloned.1.call-start = ((), (), s32[]{:S(2)}) async-start(), calls=%async_computation | async-start | bytes 13369344 | tf_op jit(solution)/shard_map/all_gather | solution.py:37
  7.3 157.9 %all-gather.5.cloned.1.call-start = ((), (), s32[]{:S(2)}) async-start(), calls=%async_computation.1 | async-start | bytes 13369344 | tf_op jit(solution)/shard_map/all_gather | solution.py:44
  14.2 13.1 %collective-permute-start.9 = (bf16[4,6,2,1,1,512]{5,3,2,1,0,4:T(2,128)(2,1)S(1)}, bf16[4,6,2,1,1,512]{5,3,2,1,0,4:T(2,128)(2,1)S(1)}, u32[]{:S(2)}, u32[]{:S(2)}) collective-permute-start(bf16[4,6,2,1,1,512]{5,3,2,1,0,4:T(2,128)(2,1)S(1)} %get-tuple-element.260), channel_id=1, source_target_pairs={{0,10},{1,11},{2,8},{3,9},{4,14},{5,15},{6,12},{7,13},{8,2},{9,3},... | collective-permute-start | bytes 147464 | tf_op jit(solution)/shard_map/ppermute | solution.py:20
  20.5 7.3 %collective-permute-start.8 = (bf16[4,6,2,1,1,512]{5,3,2,1,0,4:T(2,128)(2,1)S(1)}, bf16[4,6,2,1,1,512]{5,3,2,1,0,4:T(2,128)(2,1)S(1)}, u32[]{:S(2)}, u32[]{:S(2)}) collective-permute-start(bf16[4,6,2,1,1,512]{5,3,2,1,0,4:T(2,128)(2,1)S(1)} %get-tuple-element.261), channel_id=1, source_target_pairs={{0,9},{1,8},{2,11},{3,10},{4,13},{5,12},{6,15},{7,14},{8,1},{9,0},... | collective-permute-start | bytes 147464 | tf_op jit(solution)/shard_map/ppermute | solution.py:20
  20.6 15.5 %collective-permute-start.7 = (bf16[4,6,2,1,1,512]{5,3,2,1,0,4:T(2,128)(2,1)S(1)}, bf16[4,6,2,1,1,512]{5,3,2,1,0,4:T(2,128)(2,1)S(1)}, u32[]{:S(2)}, u32[]{:S(2)}) collective-permute-start(bf16[4,6,2,1,1,512]{5,3,2,1,0,4:T(2,128)(2,1)S(1)} %get-tuple-element.262), channel_id=1, source_target_pairs={{0,8},{1,9},{2,10},{3,11},{4,12},{5,13},{6,14},{7,15},{8,0},{9,1},... | collective-permute-start | bytes 147464 | tf_op jit(solution)/shard_map/ppermute | solution.py:20
  23.5 12.9 %collective-permute-start.6 = (bf16[4,6,2,1,1,512]{5,3,2,1,0,4:T(2,128)(2,1)S(1)}, bf16[4,6,2,1,1,512]{5,3,2,1,0,4:T(2,128)(2,1)S(1)}, u32[]{:S(2)}, u32[]{:S(2)}) collective-permute-start(bf16[4,6,2,1,1,512]{5,3,2,1,0,4:T(2,128)(2,1)S(1)} %get-tuple-element.263), channel_id=1, source_target_pairs={{0,7},{1,6},{2,5},{3,4},{4,3},{5,2},{6,1},{7,0},{8,15},{9,14},{10,... | collective-permute-start | bytes 147464 | tf_op jit(solution)/shard_map/ppermute | solution.py:20
  23.8 14.0 %collective-permute-start.5 = (bf16[4,6,2,1,1,512]{5,3,2,1,0,4:T(2,128)(2,1)S(1)}, bf16[4,6,2,1,1,512]{5,3,2,1,0,4:T(2,128)(2,1)S(1)}, u32[]{:S(2)}, u32[]{:S(2)}) collective-permute-start(bf16[4,6,2,1,1,512]{5,3,2,1,0,4:T(2,128)(2,1)S(1)} %get-tuple-element.264), channel_id=1, source_target_pairs={{0,6},{1,7},{2,4},{3,5},{4,2},{5,3},{6,0},{7,1},{8,14},{9,15},{10,... | collective-permute-start | bytes 147464 | tf_op jit(solution)/shard_map/ppermute | solution.py:20
  27.4 12.0 %collective-permute-start.4 = (bf16[4,6,2,1,1,512]{5,3,2,1,0,4:T(2,128)(2,1)S(1)}, bf16[4,6,2,1,1,512]{5,3,2,1,0,4:T(2,128)(2,1)S(1)}, u32[]{:S(2)}, u32[]{:S(2)}) collective-permute-start(bf16[4,6,2,1,1,512]{5,3,2,1,0,4:T(2,128)(2,1)S(1)} %get-tuple-element.265), channel_id=1, source_target_pairs={{0,5},{1,4},{2,7},{3,6},{4,1},{5,0},{6,3},{7,2},{8,13},{9,12},{10,... | collective-permute-start | bytes 147464 | tf_op jit(solution)/shard_map/ppermute | solution.py:20
  27.8 14.7 %collective-permute-start.3 = (bf16[4,6,2,1,1,512]{5,3,2,1,0,4:T(2,128)(2,1)S(1)}, bf16[4,6,2,1,1,512]{5,3,2,1,0,4:T(2,128)(2,1)S(1)}, u32[]{:S(2)}, u32[]{:S(2)}) collective-permute-start(bf16[4,6,2,1,1,512]{5,3,2,1,0,4:T(2,128)(2,1)S(1)} %get-tuple-element.266), channel_id=1, source_target_pairs={{0,4},{1,5},{2,6},{3,7},{4,0},{5,1},{6,2},{7,3},{8,12},{9,13},{10,... | collective-permute-start | bytes 147464 | tf_op jit(solution)/shard_map/ppermute | solution.py:20
  36.1 7.4 %collective-permute-start.2 = (bf16[4,6,2,1,1,512]{5,3,2,1,0,4:T(2,128)(2,1)S(1)}, bf16[4,6,2,1,1,512]{5,3,2,1,0,4:T(2,128)(2,1)S(1)}, u32[]{:S(2)}, u32[]{:S(2)}) collective-permute-start(bf16[4,6,2,1,1,512]{5,3,2,1,0,4:T(2,128)(2,1)S(1)} %get-tuple-element.267), channel_id=1, source_target_pairs={{0,3},{1,2},{2,1},{3,0},{4,7},{5,6},{6,5},{7,4},{8,11},{9,10},{10,... | collective-permute-start | bytes 147464 | tf_op jit(solution)/shard_map/ppermute | solution.py:20
  36.5 8.7 %collective-permute-start.1 = (bf16[4,6,2,1,1,512]{5,3,2,1,0,4:T(2,128)(2,1)S(1)}, bf16[4,6,2,1,1,512]{5,3,2,1,0,4:T(2,128)(2,1)S(1)}, u32[]{:S(2)}, u32[]{:S(2)}) collective-permute-start(bf16[4,6,2,1,1,512]{5,3,2,1,0,4:T(2,128)(2,1)S(1)} %get-tuple-element.268), channel_id=1, source_target_pairs={{0,2},{1,3},{2,0},{3,1},{4,6},{5,7},{6,4},{7,5},{8,10},{9,11},{10,... | collective-permute-start | bytes 147464 | tf_op jit(solution)/shard_map/ppermute | solution.py:20
  37.8 9.8 %collective-permute-start = (bf16[4,6,2,1,1,512]{5,3,2,1,0,4:T(2,128)(2,1)S(1)}, bf16[4,6,2,1,1,512]{5,3,2,1,0,4:T(2,128)(2,1)S(1)}, u32[]{:S(2)}, u32[]{:S(2)}) collective-permute-start(bf16[4,6,2,1,1,512]{5,3,2,1,0,4:T(2,128)(2,1)S(1)} %get-tuple-element.269), channel_id=1, source_target_pairs={{0,1},{1,0},{2,3},{3,2},{4,5},{5,4},{6,7},{7,6},{8,9},{9,8},{10,11... | collective-permute-start | bytes 147464 | tf_op jit(solution)/shard_map/ppermute | solution.py:20
  39.4 21.1 %collective-permute-start.10 = (bf16[4,6,2,1,1,512]{5,3,2,1,0,4:T(2,128)(2,1)S(1)}, bf16[4,6,2,1,1,512]{5,3,2,1,0,4:T(2,128)(2,1)S(1)}, u32[]{:S(2)}, u32[]{:S(2)}) collective-permute-start(bf16[4,6,2,1,1,512]{5,3,2,1,0,4:T(2,128)(2,1)S(1)} %get-tuple-element.259), channel_id=1, source_target_pairs={{0,11},{1,10},{2,9},{3,8},{4,15},{5,14},{6,13},{7,12},{8,3},{9,2},... | collective-permute-start | bytes 147464 | tf_op jit(solution)/shard_map/ppermute | solution.py:20
  42.4 18.9 %collective-permute-start.11 = (bf16[4,6,2,1,1,512]{5,3,2,1,0,4:T(2,128)(2,1)S(1)}, bf16[4,6,2,1,1,512]{5,3,2,1,0,4:T(2,128)(2,1)S(1)}, u32[]{:S(2)}, u32[]{:S(2)}) collective-permute-start(bf16[4,6,2,1,1,512]{5,3,2,1,0,4:T(2,128)(2,1)S(1)} %get-tuple-element.258), channel_id=1, source_target_pairs={{0,12},{1,13},{2,14},{3,15},{4,8},{5,9},{6,10},{7,11},{8,4},{9,5},... | collective-permute-start | bytes 147464 | tf_op jit(solution)/shard_map/ppermute | solution.py:20
  43.6 18.7 %collective-permute-start.12 = (bf16[4,6,2,1,1,512]{5,3,2,1,0,4:T(2,128)(2,1)S(1)}, bf16[4,6,2,1,1,512]{5,3,2,1,0,4:T(2,128)(2,1)S(1)}, u32[]{:S(2)}, u32[]{:S(2)}) collective-permute-start(bf16[4,6,2,1,1,512]{5,3,2,1,0,4:T(2,128)(2,1)S(1)} %get-tuple-element.257), channel_id=1, source_target_pairs={{0,13},{1,12},{2,15},{3,14},{4,9},{5,8},{6,11},{7,10},{8,5},{9,4},... | collective-permute-start | bytes 147464 | tf_op jit(solution)/shard_map/ppermute | solution.py:20
  45.1 18.0 %collective-permute-start.13 = (bf16[4,6,2,1,1,512]{5,3,2,1,0,4:T(2,128)(2,1)S(1)}, bf16[4,6,2,1,1,512]{5,3,2,1,0,4:T(2,128)(2,1)S(1)}, u32[]{:S(2)}, u32[]{:S(2)}) collective-permute-start(bf16[4,6,2,1,1,512]{5,3,2,1,0,4:T(2,128)(2,1)S(1)} %get-tuple-element.256), channel_id=1, source_target_pairs={{0,14},{1,15},{2,12},{3,13},{4,10},{5,11},{6,8},{7,9},{8,6},{9,7},... | collective-permute-start | bytes 147464 | tf_op jit(solution)/shard_map/ppermute | solution.py:20
  47.6 16.4 %collective-permute-start.14 = (bf16[4,6,2,1,1,512]{5,3,2,1,0,4:T(2,128)(2,1)S(1)}, bf16[4,6,2,1,1,512]{5,3,2,1,0,4:T(2,128)(2,1)S(1)}, u32[]{:S(2)}, u32[]{:S(2)}) collective-permute-start(bf16[4,6,2,1,1,512]{5,3,2,1,0,4:T(2,128)(2,1)S(1)} %get-tuple-element.255), channel_id=1, source_target_pairs={{0,15},{1,14},{2,13},{3,12},{4,11},{5,10},{6,9},{7,8},{8,7},{9,6},... | collective-permute-start | bytes 147464 | tf_op jit(solution)/shard_map/ppermute | solution.py:20
  64.8 0.9 copy-start.1
Sparse Core Ops, SparseCore 0:
  9.2 79.8 all-gather.2
  91.0 74.1 all-gather.4
